TPU v7x, 32 devices: a whole 2x2x4 slice. The times are simulated.
32 devices in a mesh: parts: 2 (over y), row: 4 (over x, core), col: 4 (over z).
Axes of the slice: x: 2, y: 2, z: 4, core: 2. Of those that a mesh axis runs over, the one named last changes fastest.
Arguments:
- latent: bfloat16 [4, 32, 32, 640], P('parts', 'row', 'col'), parts along dimension 0, may hold values from -6 to 6
- timestep: int32 [4], P('parts'), parts along dimension 0, may hold values from 0 to 999
- gn_gain: float32 [640], replicated, may hold values from 0.25 to 1.75
- gn_bias: float32 [640], replicated, may hold values from -3 to 3
- conv_weight: bfloat16 [3, 3, 640, 640], P(None, None, None, 'row'), may hold values from -0.078125 to 0.078125
- conv_bias: float32 [640], replicated, may hold values from -3 to 3
- time_weight: bfloat16 [320, 640], replicated, may hold values from -0.625 to 0.625
- ln_gain: float32 [640], replicated, may hold values from 0.25 to 1.75
- q_weight: bfloat16 [640, 384], replicated, may hold values from -0.5 to 0.5
- k_weight: bfloat16 [640, 384], replicated, may hold values from -0.25 to 0.25
- v_weight: bfloat16 [640, 384], replicated, may hold values from -0.25 to 0.25
- out_weight: bfloat16 [384, 640], replicated, may hold values from -0.3125 to 0.3125
- stale_keys: bfloat16 [4, 32, 32, 384], P('parts', 'row', 'col'), parts along dimension 0, may hold values from -40 to 40
- stale_values: bfloat16 [4, 32, 32, 384], P('parts', 'row', 'col'), parts along dimension 0, may hold values from -6 to 6
Outputs:
- mixed: bfloat16 [4, 32, 32, 640], P('parts', 'row', 'col'), parts along dimension 0
- fresh_keys: bfloat16 [4, 32, 32, 384], P('parts', 'row', 'col'), parts along dimension 0
- fresh_values: bfloat16 [4, 32, 32, 384], P('parts', 'row', 'col'), parts along dimension 0
There are 2 independent parts, one for each index of `parts`. A program takes and returns all parts, laid end to end along the dimension named above; an argument that names none is the same for every part. Nothing has to cross between parts.
All inputs are finite; a program needn't handle non-finite values.
Results may differ from a plain program's by a relative error of at most 0.012.
Values may be sent and summed in bfloat16 or wider, within the bound.
A program may use at most 64 MiB of HBM per device.

v0:
```python
import jax
import jax.numpy as jnp
from jax import lax
from jax.sharding import PartitionSpec as P

HD = 64
GROUPS = 32


def with_halo(cells, sides, width):
    for axis, dim in sides:
        count = lax.axis_size(axis)
        ends = count - 1
        head = lax.slice_in_dim(cells, 0, width, axis=dim)
        tail = lax.slice_in_dim(cells, cells.shape[dim] - width, cells.shape[dim], axis=dim)
        cells = jnp.concatenate(
            [
                lax.ppermute(tail, axis, [(i, (i + 1) % count) for i in range(ends)]),
                cells,
                lax.ppermute(head, axis, [((i + 1) % count, i) for i in range(ends)]),
            ],
            axis=dim,
        )
    return cells


def time_features(timestep, width):
    half = width // 2
    freqs = jnp.exp(-jnp.log(10000.0) * jnp.arange(half, dtype=jnp.float32) / half)
    angles = timestep.astype(jnp.float32)[:, None] * freqs[None, :]
    return jnp.concatenate([jnp.cos(angles), jnp.sin(angles)], axis=1)


def make_fold(query_all, own_query, own_key, span, heads):
    batch, rows_q, inner = query_all.shape
    head_size = inner // heads
    query_heads = query_all.reshape(batch, rows_q, heads, head_size)
    query_block = jnp.arange(rows_q, dtype=jnp.int32) // span

    def fold(carry, pieces, start):
        keys_piece, values_piece = pieces
        count = keys_piece.shape[1]
        width = 128
        keys_blocks = keys_piece.reshape(batch, count // width, width, heads, head_size).transpose(
            1, 0, 2, 3, 4
        )
        values_blocks = values_piece.reshape(
            batch, count // width, width, heads, head_size
        ).transpose(1, 0, 2, 3, 4)
        offsets = width * jnp.arange(count // width, dtype=jnp.int32)

        def step(state, items):
            peak, total, summed = state
            keys_block, values_block, offset = items
            scores = jnp.einsum(
                "bqhd,bkhd->bhqk", query_heads, keys_block, preferred_element_type=jnp.float32
            )
            key_block = (offset + jnp.arange(width, dtype=jnp.int32)) // span
            masked = (query_block == own_query)[:, None] & (key_block == own_key)[None, :]
            scores = jnp.where(masked, -1e30, scores)
            new_peak = jnp.maximum(peak, jnp.max(scores, axis=-1))
            weights = jnp.where(masked, 0.0, jnp.exp(scores - new_peak[..., None]))
            factor = jnp.exp(peak - new_peak)
            total = total * factor + jnp.sum(weights, axis=-1)
            summed = summed * factor[..., None] + jnp.einsum(
                "bhqk,bkhd->bhqd",
                weights.astype(jnp.bfloat16),
                values_block,
                preferred_element_type=jnp.float32,
            )
            return ((new_peak, total, summed), None)

        result, unused = lax.scan(step, carry, (keys_blocks, values_blocks, offsets))
        return result

    return fold


def body(
    latent,
    timestep,
    gn_gain,
    gn_bias,
    conv_weight,
    conv_bias,
    time_weight,
    ln_gain,
    q_weight,
    k_weight,
    v_weight,
    out_weight,
    stale_keys,
    stale_values,
):
    batch, rows, columns, channels = latent.shape
    inner = q_weight.shape[1]
    heads = inner // HD
    span = rows * columns
    count_all = span * lax.axis_size("row") * lax.axis_size("col") * (channels // GROUPS)
    emb = jax.nn.silu(time_features(timestep, time_weight.shape[0])).astype(jnp.bfloat16)
    temb = jnp.dot(emb, time_weight, preferred_element_type=jnp.float32)
    values = latent.astype(jnp.float32)
    grouped = values.reshape(batch, span, GROUPS, channels // GROUPS)
    sum_one = jnp.sum(grouped, axis=(1, 3))
    sum_two = jnp.sum(grouped * grouped, axis=(1, 3))
    total_one, total_two = lax.psum((sum_one, sum_two), ("row", "col"))
    mean = total_one / count_all
    var = total_two / count_all - mean * mean
    normed = (grouped - mean[:, None, :, None]) * lax.rsqrt(var + 1e-05)[:, None, :, None]
    normed = normed.reshape(batch, rows, columns, channels) * gn_gain + gn_bias
    act = jax.nn.silu(normed).astype(jnp.bfloat16)
    padded = with_halo(act, (("row", 1), ("col", 2)), 1)
    piece = lax.all_gather(conv_weight, "row", axis=3, tiled=True)
    result = jnp.zeros((batch, rows, columns, piece.shape[3]), jnp.float32)
    for down in range(3):
        for across in range(3):
            result = result + jnp.dot(
                padded[:, down : down + rows, across : across + columns, :],
                piece[down, across],
                preferred_element_type=jnp.float32,
            )
    hidden = (values + result + conv_bias + temb[:, None, None, :]).astype(jnp.bfloat16)
    hidden_f = hidden.astype(jnp.float32)
    centre = hidden_f - jnp.mean(hidden_f, axis=-1, keepdims=True)
    spread = jnp.mean(centre * centre, axis=-1, keepdims=True)
    layer_normed = (centre * lax.rsqrt(spread + 1e-05) * ln_gain).astype(jnp.bfloat16)
    queries = (
        jnp.dot(layer_normed, q_weight, preferred_element_type=jnp.float32)
        * (1.0 / jnp.sqrt(jnp.float32(HD)))
    ).astype(jnp.bfloat16)
    fresh_keys = jnp.dot(layer_normed, k_weight, preferred_element_type=jnp.float32).astype(
        jnp.bfloat16
    )
    fresh_values = jnp.dot(layer_normed, v_weight, preferred_element_type=jnp.float32).astype(
        jnp.bfloat16
    )
    query_rows = queries.reshape(batch, span, inner)
    stale_k = stale_keys.reshape(batch, span, inner)
    stale_v = stale_values.reshape(batch, span, inner)
    own_q = query_rows.reshape(batch, span, heads, HD)
    own_k = fresh_keys.reshape(batch, span, heads, HD)
    own_v = fresh_values.reshape(batch, span, heads, HD)
    own_scores = jnp.einsum("bqhd,bkhd->bhqk", own_q, own_k, preferred_element_type=jnp.float32)
    own_peak = jnp.max(own_scores, axis=-1)
    query_all = lax.all_gather(query_rows, "col", axis=1, tiled=True)
    query_index = lax.axis_index("col")
    key_index = lax.axis_index("row")
    rows_q = query_all.shape[1]
    initial = (
        jnp.full((batch, heads, rows_q), -1e30, jnp.float32),
        jnp.zeros((batch, heads, rows_q), jnp.float32),
        jnp.zeros((batch, heads, rows_q, HD), jnp.float32),
    )
    fold = make_fold(query_all, query_index, key_index, span, heads)
    peak, total, summed = fold(
        initial,
        (
            lax.all_gather(stale_k, "row", axis=1, tiled=True),
            lax.all_gather(stale_v, "row", axis=1, tiled=True),
        ),
        jnp.int32(0),
    )
    mine = lax.dynamic_slice_in_dim(peak, query_index * span, span, 2)
    raised = lax.dynamic_update_slice_in_dim(
        peak, jnp.maximum(mine, own_peak), query_index * span, 2
    )
    top = lax.pmax(raised.astype(jnp.bfloat16), "col").astype(raised.dtype)
    factor = jnp.exp(peak - top)
    scaled_sum = summed * factor[..., None]
    scaled_total = total * factor
    part_sum, part_total = (
        lax.psum_scatter(
            scaled_sum.astype(jnp.bfloat16), "col", scatter_dimension=2, tiled=True
        ).astype(jnp.float32),
        lax.psum_scatter(
            scaled_total.astype(jnp.bfloat16), "col", scatter_dimension=2, tiled=True
        ).astype(jnp.float32),
    )
    top_own = lax.dynamic_slice_in_dim(top, query_index * span, span, 2)
    own_weights = jnp.exp(own_scores - top_own[..., None])
    part_total = part_total + jnp.sum(own_weights, axis=-1)
    part_sum = part_sum + jnp.einsum(
        "bhqk,bkhd->bhqd",
        own_weights.astype(jnp.bfloat16),
        own_v,
        preferred_element_type=jnp.float32,
    )
    attn = (
        (part_sum / part_total[..., None])
        .transpose(0, 2, 1, 3)
        .reshape(batch, span, inner)
        .astype(jnp.bfloat16)
    )
    mixed = hidden_f.reshape(batch, span, channels) + jnp.dot(
        attn, out_weight, preferred_element_type=jnp.float32
    )
    mixed = mixed.astype(jnp.bfloat16).reshape(batch, rows, columns, channels)
    return (mixed, fresh_keys, fresh_values)


def solution(mesh):
    placed = (
        P("parts", "row", "col", None),
        P("parts"),
        P(),
        P(),
        P(None, None, None, "row"),
        P(),
        P(),
        P(),
        P(),
        P(),
        P(),
        P(),
        P("parts", "row", "col", None),
        P("parts", "row", "col", None),
    )
    return jax.shard_map(
        body,
        mesh=mesh,
        in_specs=placed,
        out_specs=(
            P("parts", "row", "col", None),
            P("parts", "row", "col", None),
            P("parts", "row", "col", None),
        ),
        check_vma=False,
    )
```

profile of v0, /device:TPU:0, one launch (start us, length us, event | category | flops | bytes accessed | tf_op | source)
XLA Modules:
  0.0 180.5 jit_solution(7372070736849188195)
XLA Ops:
  8.6 35.7 %all-reduce = (f32[2,32]{1,0:T(2,128)S(1)}, f32[2,32]{1,0:T(2,128)S(1)}) all-reduce(f32[2,32]{1,0:T(2,128)S(1)} %reduce_sum.76, f32[2,32]{1,0:T(2,128)S(1)} %reduce_sum.73), channel_id=1, replica_groups=mesh['parts'=2,'row'=4,'col'=4] {'row','col'}, use_global_device_ids=true, to_apply=%region_5.6 | all-reduce | flops 128 | bytes 1024 | tf_op jit(solution)/shard_map/psum | solution.py:106
  44.9 1.3 collective-permute-start
  46.2 1.3 collective-permute-start.1
  47.8 10.8 %all_gather.13 = bf16[2,256,384]{2,0,1:T(2,128)(2,1)S(1)} all-gather(bf16[2,64,384]{2,0,1:T(2,128)(2,1)S(1)} %bitcast.148), channel_id=1, replica_groups=mesh['parts'=2,'row'=4,'col'=4] {'row'}, dimensions={1}, use_global_device_ids=true | all-gather | bytes 491520 | tf_op jit(solution)/shard_map/all_gather | solution.py:158
  58.9 9.1 %all_gather.15 = bf16[2,256,384]{2,0,1:T(2,128)(2,1)S(1)} all-gather(bf16[2,64,384]{2,0,1:T(2,128)(2,1)S(1)} %bitcast.147), channel_id=1, replica_groups=mesh['parts'=2,'row'=4,'col'=4] {'row'}, dimensions={1}, use_global_device_ids=true | all-gather | bytes 491520 | tf_op jit(solution)/shard_map/all_gather | solution.py:159
  68.0 1.3 collective-permute-start.2
  69.3 1.3 collective-permute-start.3
  72.7 0.8 copy.54
  73.5 1.8 %collective-permute-done.3 = bf16[2,10,1,640]{3,2,1,0:T(2,128)(2,1)S(1)} collective-permute-done((bf16[2,10,1,640]{3,2,1,0:T(2,128)(2,1)S(1)}, bf16[2,10,1,640]{3,2,1,0:T(2,128)(2,1)S(1)}, u32[]{:S(2)}, u32[]{:S(2)}) %collective-permute-start.3) | collective-permute-done | bytes 25632 | tf_op jit(solution)/shard_map/ppermute | solution.py:20
  75.6 1.5 fusion.41
  77.1 1.5 fusion.38
  78.6 1.5 fusion.39
  80.1 1.5 fusion.37
  81.6 1.5 fusion.40
  83.1 1.5 fusion.35
  84.7 1.5 fusion.36
  86.2 1.5 fusion.21
  87.7 1.7 fusion.86
  90.7 0.9 reshape.105
  91.5 1.3 fusion.34
  92.8 0.9 reshape_reshape.3
  93.7 15.4 %all_gather.14 = bf16[2,256,384]{2,1,0:T(8,128)(2,1)S(1)} all-gather(bf16[2,64,384]{2,1,0:T(8,128)(2,1)S(1)} %bitcast.145), channel_id=1, replica_groups=mesh['parts'=2,'row'=4,'col'=4] {'col'}, dimensions={1}, use_global_device_ids=true | all-gather | bytes 491520 | tf_op jit(solution)/shard_map/all_gather | solution.py:145
  109.3 8.7 %while.17 = (s32[]{:T(128)}, f32[2,6,256]{2,1,0:T(8,128)S(1)}, f32[2,6,256]{2,1,0:T(8,128)S(1)}, f32[2,6,256,64]{2,3,1,0:T(8,128)S(1)}, s32[]{:T(128)}, /*index=...) while((s32[]{:T(128)}, f32[2,6,256]{2,1,0:T(8,128)S(1)}, ...), condition=%wide.region_11.12_spmd.clone, body=%wide.region_8.11_spmd.clone.sunk | while | flops 104451456 | bytes 8988089 | solution.py:73
  110.7 1.4 fusion.108
  115.0 1.4 fusion.108
  117.9 1.3 fusion.87
  119.5 8.7 %pmax.7 = bf16[2,6,256]{2,1,0:T(8,128)(2,1)S(1)} all-reduce(bf16[2,6,256]{2,1,0:T(8,128)(2,1)S(1)} %convert_element_type.78), channel_id=1, replica_groups=mesh['parts'=2,'row'=4,'col'=4] {'col'}, use_global_device_ids=true, to_apply=%region_13.14 | all-reduce | flops 3072 | bytes 12288 | tf_op jit(solution)/shard_map/pmax | solution.py:167
  129.8 1.4 multiply_convert_fusion
  131.8 15.8 %reduce-scatter.7.cloned.1.call-done = bf16[64,12]{1,0:T(8,128)(2,1)} async-done(((bf16[256,12]{1,0:T(8,128)(2,1)}), bf16[64,12]{1,0:T(8,128)(2,1)}) %reduce-scatter.7.cloned.1.call-update) | async-done | bytes 1552
  148.5 23.0 %reduce-scatter.5.cloned.1.call-done = bf16[2,6,64,64]{3,2,1,0:T(8,128)(2,1)} async-done(((bf16[2,6,256,64]{3,2,1,0:T(8,128)(2,1)}), bf16[2,6,64,64]{3,2,1,0:T(8,128)(2,1)}) %reduce-scatter.5.cloned.1.call-update) | async-done | bytes 98320 | tf_op jit(solution)/shard_map/reduce_scatter | solution.py:172
  171.4 1.2 fusion.32
  173.0 0.9 fusion.33
  (117 shorter events, 15.5 us)
Async XLA Ops:
  7.2 165.9 %copy-start = (bf16[384,640]{1,0:T(8,128)(2,1)S(1)}, bf16[384,640]{1,0:T(8,128)(2,1)}, u32[]{:S(2)}) copy-start(bf16[384,640]{1,0:T(8,128)(2,1)} %param.27) | copy-start | bytes 1474564
  7.2 1.0 copy-start.4
  7.2 37.6 %copy-start.13 = (f32[640]{0:T(1024)S(1)}, f32[640]{0:T(1024)}, u32[]{:S(2)}) copy-start(f32[640]{0:T(1024)} %param.18) | copy-start | bytes 7684
  7.2 37.6 %copy-start.12 = (f32[640]{0:T(1024)S(1)}, f32[640]{0:T(1024)}, u32[]{:S(2)}) copy-start(f32[640]{0:T(1024)} %param.19) | copy-start | bytes 7684
  7.2 40.3 %copy-start.16 = (s32[2]{0:T(128)S(1)}, s32[2]{0:T(128)}, u32[]{:S(2)}) copy-start(s32[2]{0:T(128)} %param.17) | copy-start | bytes 28
  7.2 40.3 %copy-start.10 = (bf16[2,8,8,384]{3,2,1,0:T(8,128)(2,1)S(1)}, bf16[2,8,8,384]{3,2,1,0:T(8,128)(2,1)}, u32[]{:S(2)}) copy-start(bf16[2,8,8,384]{3,2,1,0:T(8,128)(2,1)} %param.28) | copy-start | bytes 294916
  7.2 40.4 %copy-start.11 = (bf16[2,8,8,384]{3,2,1,0:T(8,128)(2,1)S(1)}, bf16[2,8,8,384]{3,2,1,0:T(8,128)(2,1)}, u32[]{:S(2)}) copy-start(bf16[2,8,8,384]{3,2,1,0:T(8,128)(2,1)} %param.29) | copy-start | bytes 294916
  7.2 51.4 %copy-start.7 = (bf16[320,640]{1,0:T(8,128)(2,1)S(1)}, bf16[320,640]{1,0:T(8,128)(2,1)}, u32[]{:S(2)}) copy-start(bf16[320,640]{1,0:T(8,128)(2,1)} %param.22) | copy-start | bytes 1228804
  7.3 68.3 %all-gather.2.cloned.1.call-start = ((), (), s32[]{:S(2)}) async-start(), calls=%async_computation.2 | async-start | bytes 9216000 | tf_op jit(solution)/shard_map/all_gather | solution.py:113
  8.0 139.6 %reduce-scatter.7.cloned.1.call-start = ((), (), s32[]{:S(2)}) async-start(), calls=%async_computation.4 | async-start | bytes 81920
  44.9 23.0 %collective-permute-start = (bf16[2,1,8,640]{3,2,1,0:T(8,128)(2,1)S(1)}, bf16[2,1,8,640]{3,2,1,0:T(8,128)(2,1)S(1)}, u32[]{:S(2)}, u32[]{:S(2)}) collective-permute-start(bf16[2,1,8,640]{3,2,1,0:T(8,128)(2,1)S(1)} %get-tuple-element.235), channel_id=1, source_target_pairs={{0,4},{4,8},{8,12},{1,5},{5,9},{9,13},{2,6},{6,10},{10,14},{3,7},{... | collective-permute-start | bytes 61448 | tf_op jit(solution)/shard_map/ppermute | solution.py:18
  46.2 21.7 %collective-permute-start.1 = (bf16[2,1,8,640]{3,2,1,0:T(8,128)(2,1)S(1)}, bf16[2,1,8,640]{3,2,1,0:T(8,128)(2,1)S(1)}, u32[]{:S(2)}, u32[]{:S(2)}) collective-permute-start(bf16[2,1,8,640]{3,2,1,0:T(8,128)(2,1)S(1)} %get-tuple-element.236), channel_id=1, source_target_pairs={{4,0},{8,4},{12,8},{5,1},{9,5},{13,9},{6,2},{10,6},{14,10},{7,3},{... | collective-permute-start | bytes 61448 | tf_op jit(solution)/shard_map/ppermute | solution.py:20
  68.0 5.5 %collective-permute-start.2 = (bf16[2,10,1,640]{3,2,1,0:T(2,128)(2,1)S(1)}, bf16[2,10,1,640]{3,2,1,0:T(2,128)(2,1)S(1)}, u32[]{:S(2)}, u32[]{:S(2)}) collective-permute-start(bf16[2,10,1,640]{3,2,1,0:T(2,128)(2,1)S(1)} %get-tuple-element.233), channel_id=1, source_target_pairs={{0,1},{1,2},{2,3},{4,5},{5,6},{6,7},{8,9},{9,10},{10,11},{12,13},{... | collective-permute-start | bytes 76808 | tf_op jit(solution)/shard_map/ppermute | solution.py:18
  69.3 6.0 %collective-permute-start.3 = (bf16[2,10,1,640]{3,2,1,0:T(2,128)(2,1)S(1)}, bf16[2,10,1,640]{3,2,1,0:T(2,128)(2,1)S(1)}, u32[]{:S(2)}, u32[]{:S(2)}) collective-permute-start(bf16[2,10,1,640]{3,2,1,0:T(2,128)(2,1)S(1)} %get-tuple-element.234), channel_id=1, source_target_pairs={{1,0},{2,1},{3,2},{5,4},{6,5},{7,6},{9,8},{10,9},{11,10},{13,12},{... | collective-permute-start | bytes 76808 | tf_op jit(solution)/shard_map/ppermute | solution.py:20
  86.2 1.5 copy-start.14
  87.7 1.9 %copy-start.15 = (f32[640]{0:T(1024)S(1)}, f32[640]{0:T(1024)}, u32[]{:S(2)}) copy-start(f32[640]{0:T(1024)} %param.23) | copy-start | bytes 7684
  87.7 2.0 %copy-start.5 = (bf16[640,384]{1,0:T(8,128)(2,1)S(1)}, bf16[640,384]{1,0:T(8,128)(2,1)}, u32[]{:S(2)}) copy-start(bf16[640,384]{1,0:T(8,128)(2,1)} %param.25) | copy-start | bytes 1474564
  89.4 19.7 %copy-start.1 = (f32[2,8,8,640]{3,2,1,0:T(8,128)}, f32[2,8,8,640]{3,2,1,0:T(8,128)S(1)}, u32[]{:S(2)}) copy-start(f32[2,8,8,640]{3,2,1,0:T(8,128)S(1)} %get-tuple-element.242) | copy-start | bytes 983044
  90.0 0.6 copy-start.8
  112.1 1.0 copy-start.3
  116.4 1.0 copy-start.3
  129.2 42.2 %reduce-scatter.5.cloned.1.call-start = ((), (), s32[]{:S(2)}) async-start(), calls=%async_computation.3 | async-start | bytes 983040 | tf_op jit(solution)/shard_map/reduce_scatter | solution.py:172
  129.7 1.4 copy-start.6
  131.4 41.4 %copy-start.9 = (bf16[2,8,8,384]{3,2,1,0:T(8,128)(2,1)}, bf16[2,8,8,384]{3,2,1,0:T(8,128)(2,1)S(1)}, u32[]{:S(2)}) copy-start(bf16[2,8,8,384]{3,2,1,0:T(8,128)(2,1)S(1)} %convolution_convert_fusion) | copy-start | bytes 294916
  131.8 41.3 %copy-start.2 = (f32[2,8,8,640]{3,2,1,0:T(8,128)S(1)}, f32[2,8,8,640]{3,2,1,0:T(8,128)}, u32[]{:S(2)}) copy-start(f32[2,8,8,640]{3,2,1,0:T(8,128)} %copy-done.1) | copy-start | bytes 983044
Sparse Core Ops, SparseCore 0:
  9.6 59.9 all-gather.1
  129.3 18.1 reduce-scatter.6
  150.0 21.4 reduce-scatter.4
where the time goes:
time: 181 us
  blocking collectives  79.7 us (44%)
  waiting for transfers between devices  41.3 us (23%)
  matrix products  22.8 us (13%)
  between operations  14.4 us (8%)
  local copies, waits for them, and re-layouts  12 us (7%)
  starting transfers between devices  5.28 us (3%)
  other arithmetic  4.77 us (3%)
    psum x1, blocking collectives, body(): total_one, total_two = lax.psum((sum_one, sum_two), ('row', 'col'))  35.7 us
    reduce_scatter x1, waiting for transfers between devices, body(): lax.psum_scatter(scaled_sum.astype(jnp.bfloat16), 'col', scatter_dimensio...  23 us
    unnamed x4, waiting for transfers between devices  16.5 us
    all_gather x1, blocking collectives, body(): query_all = lax.all_gather(query_rows, 'col', axis=1, tiled=True)  15.4 us
    dot_general x9, matrix products, body(): jnp.dot(padded[:, down:down + rows, across:across + columns, :], piece[do...  13.7 us
    all_gather x1, blocking collectives, body(): lax.all_gather(stale_k, 'row', axis=1, tiled=True)  10.8 us
    all_gather x1, blocking collectives, body(): lax.all_gather(stale_v, 'row', axis=1, tiled=True)  9.07 us
    pmax x1, blocking collectives, body(): top = lax.pmax(raised.astype(jnp.bfloat16), 'col').astype(raised.dtype)  8.73 us
  transfers between devices with their start and end apart: 7, of which 3 were waited for; matrix products, arithmetic and copies ran while one was open for 4% of the time, Pallas kernels for 0%

commit v1 on v0

--- a/solution.py
+++ b/solution.py
@@ -5,6 +5,12 @@
 
 HD = 64
 GROUPS = 32
+
+
+def _find_views(slab_in):
+    for pp in ("col", "row"):
+        slab_in = lax.psum(slab_in, axis_name=pp)
+    return slab_in
 
 
 def with_halo(cells, sides, width):
@@ -103,7 +109,7 @@
     grouped = values.reshape(batch, span, GROUPS, channels // GROUPS)
     sum_one = jnp.sum(grouped, axis=(1, 3))
     sum_two = jnp.sum(grouped * grouped, axis=(1, 3))
-    total_one, total_two = lax.psum((sum_one, sum_two), ("row", "col"))
+    total_one, total_two = _find_views((sum_one, sum_two))
     mean = total_one / count_all
     var = total_two / count_all - mean * mean
     normed = (grouped - mean[:, None, :, None]) * lax.rsqrt(var + 1e-05)[:, None, :, None]

time: 181 us -> 177 us (0.978)
  blocking collectives: 79.7 us -> 67.6 us
  waiting for transfers between devices: 41.3 us -> 48.7 us
    psum x1 -> x2, blocking collectives: 35.7 us -> 19.6 us  [_find_views(): slab_in = lax.psum(slab_in, axis_name=pp)]
    all_gather x1, waiting for transfers between devices: 0.02 us -> 9.15 us  [body(): piece = lax.all_gather(conv_weight, 'row', axis=3, tiled=True)]
    pmax x1, blocking collectives: 8.73 us -> 12.8 us  [body(): top = lax.pmax(raised.astype(jnp.bfloat16), 'col').astype(raised.dtype)]
  transfers between devices with their start and end apart: 7 -> 7, of which waited for: 3 -> 4; matrix products, arithmetic and copies ran while one was open for 4% -> 4% of each run, Pallas kernels for 0% -> 0%
where the time goes in v1:
time: 177 us; the launch traced here: 176 us
  blocking collectives  67.6 us (38%)
  waiting for transfers between devices  48.7 us (28%)
  matrix products  22.8 us (13%)
  between operations  14.4 us (8%)
  local copies, waits for them, and re-layouts  12.1 us (7%)
  starting transfers between devices  5.33 us (3%)
  other arithmetic  4.88 us (3%)
    reduce_scatter x1, waiting for transfers between devices, body(): lax.psum_scatter(scaled_sum.astype(jnp.bfloat16), 'col', scatter_dimensio...  23 us
    psum x2, blocking collectives, _find_views(): slab_in = lax.psum(slab_in, axis_name=pp)  19.6 us
    unnamed x4, waiting for transfers between devices  14.8 us
    all_gather x1, blocking collectives, body(): query_all = lax.all_gather(query_rows, 'col', axis=1, tiled=True)  14.6 us
    dot_general x9, matrix products, body(): jnp.dot(padded[:, down:down + rows, across:across + columns, :], piece[do...  13.7 us
    pmax x1, blocking collectives, body(): top = lax.pmax(raised.astype(jnp.bfloat16), 'col').astype(raised.dtype)  12.8 us
    all_gather x1, blocking collectives, body(): lax.all_gather(stale_k, 'row', axis=1, tiled=True)  11.6 us
    all_gather x1, waiting for transfers between devices, body(): piece = lax.all_gather(conv_weight, 'row', axis=3, tiled=True)  9.15 us
  transfers between devices with their start and end apart: 7, of which 4 were waited for; matrix products, arithmetic and copies ran while one was open for 4% of the time, Pallas kernels for 0%

profile of v1, /device:TPU:0, one launch (start us, length us, event | category | flops | bytes accessed | tf_op | source)
XLA Modules:
  0.0 176.0 jit_solution(8458504265856511704)
XLA Ops:
  8.6 13.4 %all-reduce = (f32[2,32]{1,0:T(2,128)S(1)}, f32[2,32]{1,0:T(2,128)S(1)}) all-reduce(f32[2,32]{1,0:T(2,128)S(1)} %reduce_sum.76, f32[2,32]{1,0:T(2,128)S(1)} %reduce_sum.73), channel_id=1, replica_groups=mesh['parts'=2,'row'=4,'col'=4] {'col'}, use_global_device_ids=true, to_apply=%region_6.7 | all-reduce | flops 128 | bytes 1024 | tf_op jit(solution)/shard_map/psum | solution.py:12
  22.1 6.2 %all-reduce.1 = (f32[2,32]{1,0:T(2,128)S(1)}, f32[2,32]{1,0:T(2,128)S(1)}) all-reduce(f32[2,32]{1,0:T(2,128)S(1)} %get-tuple-element.223, f32[2,32]{1,0:T(2,128)S(1)} %get-tuple-element.224), channel_id=1, replica_groups=mesh['parts'=2,'row'=4,'col'=4] {'row'}, use_global_device_ids=true, to_apply=%region_7.8 | all-reduce | flops 128 | bytes 1024 | tf_op jit(solution)/shard_map/psum | solution.py:12
  28.8 1.3 collective-permute-start
  30.1 1.3 collective-permute-start.1
  31.7 11.6 %all_gather.13 = bf16[2,256,384]{2,0,1:T(2,128)(2,1)S(1)} all-gather(bf16[2,64,384]{2,0,1:T(2,128)(2,1)S(1)} %bitcast.148), channel_id=1, replica_groups=mesh['parts'=2,'row'=4,'col'=4] {'row'}, dimensions={1}, use_global_device_ids=true | all-gather | bytes 491520 | tf_op jit(solution)/shard_map/all_gather | solution.py:164
  43.7 9.1 %all_gather.15 = bf16[2,256,384]{2,0,1:T(2,128)(2,1)S(1)} all-gather(bf16[2,64,384]{2,0,1:T(2,128)(2,1)S(1)} %bitcast.147), channel_id=1, replica_groups=mesh['parts'=2,'row'=4,'col'=4] {'row'}, dimensions={1}, use_global_device_ids=true | all-gather | bytes 491520 | tf_op jit(solution)/shard_map/all_gather | solution.py:165
  52.8 1.3 collective-permute-start.2
  54.1 1.3 collective-permute-start.3
  58.3 1.8 %collective-permute-done.3 = bf16[2,10,1,640]{3,2,1,0:T(2,128)(2,1)S(1)} collective-permute-done((bf16[2,10,1,640]{3,2,1,0:T(2,128)(2,1)S(1)}, bf16[2,10,1,640]{3,2,1,0:T(2,128)(2,1)S(1)}, u32[]{:S(2)}, u32[]{:S(2)}) %collective-permute-start.3) | collective-permute-done | bytes 25632 | tf_op jit(solution)/shard_map/ppermute | solution.py:26
  60.3 9.1 %all-gather.2.cloned.1.call-done = bf16[3,3,640,640]{2,3,1,0:T(8,128)(2,1)} async-done(((bf16[3,3,640,160]{2,3,1,0:T(8,128)(2,1)}), bf16[3,3,640,640]{2,3,1,0:T(8,128)(2,1)}) %all-gather.2.cloned.1.call-update) | async-done | bytes 7372816 | tf_op jit(solution)/shard_map/all_gather | solution.py:119
  69.5 1.5 fusion.41
  71.0 1.5 fusion.38
  72.5 1.5 fusion.39
  74.0 1.5 fusion.37
  75.5 1.5 fusion.40
  77.0 1.5 fusion.35
  78.5 1.5 fusion.36
  80.1 1.5 fusion.21
  81.6 1.7 fusion.86
  85.4 1.3 fusion.34
  86.7 0.9 reshape_reshape.3
  87.6 14.6 %all_gather.14 = bf16[2,256,384]{2,1,0:T(8,128)(2,1)S(1)} all-gather(bf16[2,64,384]{2,1,0:T(8,128)(2,1)S(1)} %bitcast.145), channel_id=1, replica_groups=mesh['parts'=2,'row'=4,'col'=4] {'col'}, dimensions={1}, use_global_device_ids=true | all-gather | bytes 491520 | tf_op jit(solution)/shard_map/all_gather | solution.py:151
  102.3 8.8 %while.17 = (s32[]{:T(128)}, f32[2,6,256]{2,1,0:T(8,128)S(1)}, f32[2,6,256]{2,1,0:T(8,128)S(1)}, f32[2,6,256,64]{2,3,1,0:T(8,128)S(1)}, s32[]{:T(128)}, /*index=...) while((s32[]{:T(128)}, f32[2,6,256]{2,1,0:T(8,128)S(1)}, ...), condition=%wide.region_13.14_spmd.clone, body=%wide.region_10.13_spmd.clone.sunk | while | flops 104451456 | bytes 8988089 | solution.py:79
  103.8 1.4 fusion.108
  108.2 1.4 fusion.108
  111.1 1.3 fusion.87
  112.7 12.8 %pmax.7 = bf16[2,6,256]{2,1,0:T(8,128)(2,1)S(1)} all-reduce(bf16[2,6,256]{2,1,0:T(8,128)(2,1)S(1)} %convert_element_type.78), channel_id=1, replica_groups=mesh['parts'=2,'row'=4,'col'=4] {'col'}, use_global_device_ids=true, to_apply=%region_15.16 | all-reduce | flops 3072 | bytes 12288 | tf_op jit(solution)/shard_map/pmax | solution.py:173
  127.0 1.4 multiply_convert_fusion
  129.0 14.0 %reduce-scatter.7.cloned.1.call-done = bf16[64,12]{1,0:T(8,128)(2,1)} async-done(((bf16[256,12]{1,0:T(8,128)(2,1)}), bf16[64,12]{1,0:T(8,128)(2,1)}) %reduce-scatter.7.cloned.1.call-update) | async-done | bytes 1552
  144.0 23.0 %reduce-scatter.5.cloned.1.call-done = bf16[2,6,64,64]{3,2,1,0:T(8,128)(2,1)} async-done(((bf16[2,6,256,64]{3,2,1,0:T(8,128)(2,1)}), bf16[2,6,64,64]{3,2,1,0:T(8,128)(2,1)}) %reduce-scatter.5.cloned.1.call-update) | async-done | bytes 98320 | tf_op jit(solution)/shard_map/reduce_scatter | solution.py:178
  167.0 1.2 fusion.32
  168.6 0.9 fusion.33
  (118 shorter events, 17.3 us)
Async XLA Ops:
  7.2 161.4 %copy-start = (bf16[384,640]{1,0:T(8,128)(2,1)S(1)}, bf16[384,640]{1,0:T(8,128)(2,1)}, u32[]{:S(2)}) copy-start(bf16[384,640]{1,0:T(8,128)(2,1)} %param.27) | copy-start | bytes 1474564
  7.2 1.0 copy-start.4
  7.2 21.4 %copy-start.13 = (f32[640]{0:T(1024)S(1)}, f32[640]{0:T(1024)}, u32[]{:S(2)}) copy-start(f32[640]{0:T(1024)} %param.18) | copy-start | bytes 7684
  7.2 21.4 %copy-start.12 = (f32[640]{0:T(1024)S(1)}, f32[640]{0:T(1024)}, u32[]{:S(2)}) copy-start(f32[640]{0:T(1024)} %param.19) | copy-start | bytes 7684
  7.2 24.2 %copy-start.16 = (s32[2]{0:T(128)S(1)}, s32[2]{0:T(128)}, u32[]{:S(2)}) copy-start(s32[2]{0:T(128)} %param.17) | copy-start | bytes 28
  7.2 24.2 %copy-start.10 = (bf16[2,8,8,384]{3,2,1,0:T(8,128)(2,1)S(1)}, bf16[2,8,8,384]{3,2,1,0:T(8,128)(2,1)}, u32[]{:S(2)}) copy-start(bf16[2,8,8,384]{3,2,1,0:T(8,128)(2,1)} %param.28) | copy-start | bytes 294916
  7.2 24.3 %copy-start.11 = (bf16[2,8,8,384]{3,2,1,0:T(8,128)(2,1)S(1)}, bf16[2,8,8,384]{3,2,1,0:T(8,128)(2,1)}, u32[]{:S(2)}) copy-start(bf16[2,8,8,384]{3,2,1,0:T(8,128)(2,1)} %param.29) | copy-start | bytes 294916
  7.2 36.2 %copy-start.7 = (bf16[320,640]{1,0:T(8,128)(2,1)S(1)}, bf16[320,640]{1,0:T(8,128)(2,1)}, u32[]{:S(2)}) copy-start(bf16[320,640]{1,0:T(8,128)(2,1)} %param.22) | copy-start | bytes 1228804
  7.3 62.2 %all-gather.2.cloned.1.call-start = ((), (), s32[]{:S(2)}) async-start(), calls=%async_computation.2 | async-start | bytes 9216000 | tf_op jit(solution)/shard_map/all_gather | solution.py:119
  8.0 135.1 %reduce-scatter.7.cloned.1.call-start = ((), (), s32[]{:S(2)}) async-start(), calls=%async_computation.4 | async-start | bytes 81920
  28.8 24.0 %collective-permute-start = (bf16[2,1,8,640]{3,2,1,0:T(8,128)(2,1)S(1)}, bf16[2,1,8,640]{3,2,1,0:T(8,128)(2,1)S(1)}, u32[]{:S(2)}, u32[]{:S(2)}) collective-permute-start(bf16[2,1,8,640]{3,2,1,0:T(8,128)(2,1)S(1)} %get-tuple-element.237), channel_id=1, source_target_pairs={{0,4},{4,8},{8,12},{1,5},{5,9},{9,13},{2,6},{6,10},{10,14},{3,7},{... | collective-permute-start | bytes 61448 | tf_op jit(solution)/shard_map/ppermute | solution.py:24
  30.1 22.6 %collective-permute-start.1 = (bf16[2,1,8,640]{3,2,1,0:T(8,128)(2,1)S(1)}, bf16[2,1,8,640]{3,2,1,0:T(8,128)(2,1)S(1)}, u32[]{:S(2)}, u32[]{:S(2)}) collective-permute-start(bf16[2,1,8,640]{3,2,1,0:T(8,128)(2,1)S(1)} %get-tuple-element.238), channel_id=1, source_target_pairs={{4,0},{8,4},{12,8},{5,1},{9,5},{13,9},{6,2},{10,6},{14,10},{7,3},{... | collective-permute-start | bytes 61448 | tf_op jit(solution)/shard_map/ppermute | solution.py:26
  52.8 5.5 %collective-permute-start.2 = (bf16[2,10,1,640]{3,2,1,0:T(2,128)(2,1)S(1)}, bf16[2,10,1,640]{3,2,1,0:T(2,128)(2,1)S(1)}, u32[]{:S(2)}, u32[]{:S(2)}) collective-permute-start(bf16[2,10,1,640]{3,2,1,0:T(2,128)(2,1)S(1)} %get-tuple-element.235), channel_id=1, source_target_pairs={{0,1},{1,2},{2,3},{4,5},{5,6},{6,7},{8,9},{9,10},{10,11},{12,13},{... | collective-permute-start | bytes 76808 | tf_op jit(solution)/shard_map/ppermute | solution.py:24
  54.1 6.0 %collective-permute-start.3 = (bf16[2,10,1,640]{3,2,1,0:T(2,128)(2,1)S(1)}, bf16[2,10,1,640]{3,2,1,0:T(2,128)(2,1)S(1)}, u32[]{:S(2)}, u32[]{:S(2)}) collective-permute-start(bf16[2,10,1,640]{3,2,1,0:T(2,128)(2,1)S(1)} %get-tuple-element.236), channel_id=1, source_target_pairs={{1,0},{2,1},{3,2},{5,4},{6,5},{7,6},{9,8},{10,9},{11,10},{13,12},{... | collective-permute-start | bytes 76808 | tf_op jit(solution)/shard_map/ppermute | solution.py:26
  80.0 1.5 copy-start.14
  81.6 1.9 %copy-start.15 = (f32[640]{0:T(1024)S(1)}, f32[640]{0:T(1024)}, u32[]{:S(2)}) copy-start(f32[640]{0:T(1024)} %param.23) | copy-start | bytes 7684
  81.6 2.0 %copy-start.5 = (bf16[640,384]{1,0:T(8,128)(2,1)S(1)}, bf16[640,384]{1,0:T(8,128)(2,1)}, u32[]{:S(2)}) copy-start(bf16[640,384]{1,0:T(8,128)(2,1)} %param.25) | copy-start | bytes 1474564
  83.3 18.9 %copy-start.1 = (f32[2,8,8,640]{3,2,1,0:T(8,128)}, f32[2,8,8,640]{3,2,1,0:T(8,128)S(1)}, u32[]{:S(2)}) copy-start(f32[2,8,8,640]{3,2,1,0:T(8,128)S(1)} %get-tuple-element.244) | copy-start | bytes 983044
  83.9 0.6 copy-start.8
  105.2 1.0 copy-start.3
  109.6 1.0 copy-start.3
  126.5 40.5 %reduce-scatter.5.cloned.1.call-start = ((), (), s32[]{:S(2)}) async-start(), calls=%async_computation.3 | async-start | bytes 983040 | tf_op jit(solution)/shard_map/reduce_scatter | solution.py:178
  127.0 1.4 copy-start.6
  128.7 39.7 %copy-start.9 = (bf16[2,8,8,384]{3,2,1,0:T(8,128)(2,1)}, bf16[2,8,8,384]{3,2,1,0:T(8,128)(2,1)S(1)}, u32[]{:S(2)}) copy-start(bf16[2,8,8,384]{3,2,1,0:T(8,128)(2,1)S(1)} %convolution_convert_fusion) | copy-start | bytes 294916
  129.0 39.5 %copy-start.2 = (f32[2,8,8,640]{3,2,1,0:T(8,128)S(1)}, f32[2,8,8,640]{3,2,1,0:T(8,128)}, u32[]{:S(2)}) copy-start(f32[2,8,8,640]{3,2,1,0:T(8,128)} %copy-done.1) | copy-start | bytes 983044
Sparse Core Ops, SparseCore 0:
  9.6 59.7 all-gather.1
  126.6 16.4 reduce-scatter.6
  145.5 21.4 reduce-scatter.4
